TPU v7x, 32 devices: a whole 2x2x4 slice. The times are simulated.
32 devices in a mesh: row: 4 (over y, x), seq: 8 (over z, core).
Axes of the slice: x: 2, y: 2, z: 4, core: 2. Of those that a mesh axis runs over, the one named last changes fastest.
Arguments:
- hidden_in: bfloat16 [4, 1024, 2048], P('row', 'seq'), may hold values from -6 to 6
- positions: int32 [4, 1024], P('row', 'seq'), may hold values from 0 to 7164, as said below
- languages: int32 [4], replicated, may hold values from 0 to 6
- ln1_gain: bfloat16 [2048], replicated, may hold values from 0.5 to 1.5
- ln1_bias: bfloat16 [2048], replicated, may hold values from -1.1953125 to 1.1953125
- w_qkv: bfloat16 [2048, 6144], P(None, 'seq'), may hold values from -0.125 to 0.125
- b_qkv: bfloat16 [6144], P('seq'), may hold values from -1.1953125 to 1.1953125
- w_out: bfloat16 [2048, 2048], P('seq'), may hold values from -3 to 3
- ln2_gain: bfloat16 [2048], replicated, may hold values from 0.5 to 1.5
- ln2_bias: bfloat16 [2048], replicated, may hold values from -1.1953125 to 1.1953125
- w_gate: bfloat16 [2048, 5632], P(None, 'seq'), may hold values from -0.125 to 0.125
- w_up: bfloat16 [2048, 5632], P(None, 'seq'), may hold values from -0.125 to 0.125
- w_down: bfloat16 [5632, 2048], P('seq'), may hold values from -0.078125 to 0.078125
- cotangent: bfloat16 [4, 1024, 2048], P('row', 'seq'), may hold values from -6 to 6
Outputs:
- output: bfloat16 [4, 1024, 2048], P('row', 'seq')
- input_grad: bfloat16 [4, 1024, 2048], P('row', 'seq')
- grad_ln1_gain: float32 [2048], P('seq')
- grad_ln1_bias: float32 [2048], P('seq')
- grad_w_qkv: float32 [2048, 6144], P(None, 'seq')
- grad_b_qkv: float32 [6144], P('seq')
- grad_w_out: float32 [2048, 2048], P('seq')
- grad_ln2_gain: float32 [2048], P('seq')
- grad_ln2_bias: float32 [2048], P('seq')
- grad_w_gate: float32 [2048, 5632], P(None, 'seq')
- grad_w_up: float32 [2048, 5632], P(None, 'seq')
- grad_w_down: float32 [5632, 2048], P('seq')
Inputs may be any that keep to these rules, and one draw needn't show every extreme that they name: Each sequence's positions start at an offset of 0 to 4095 and rise by 1 to 3 from one token to the next; some sequence starts at 0, and another starts at 4095 and rises by 3 at every token.
All inputs are finite; a program needn't handle non-finite values.
Results may differ from a plain program's by a relative error of at most 0.013.
Values may be sent and summed in bfloat16 or wider, within the bound.
No kernel may reach another device: no remote copies, remote signals or barrier semaphores. Data moves between devices by JAX's collectives and lax.ppermute only.
A program may use at most 256 MiB of HBM per device.

v0:
```python
import jax
import jax.numpy as jnp
from jax import lax
from jax.sharding import PartitionSpec as P

HEAD_DIM = 64
ROT = 16
LANGS = 7
EPS = 1e-05
NEG = -1e30
BASE = 10000.0


def rotate(tensor, places, direction):
    half_rot = ROT // 2
    freqs = BASE ** (-(jnp.arange(half_rot, dtype=jnp.float32) * 2.0) / ROT)
    angles = places.astype(jnp.float32)[:, None] * freqs[None, :]
    cosine = jnp.cos(angles)[:, None, :]
    sine = jnp.sin(angles)[:, None, :] * direction
    first_half = tensor[..., :half_rot]
    second_half = tensor[..., half_rot:ROT]
    return jnp.concatenate(
        [
            first_half * cosine - second_half * sine,
            second_half * cosine + first_half * sine,
            tensor[..., ROT:],
        ],
        axis=-1,
    )


def standardize(values):
    center = values - jnp.mean(values, -1, keepdims=True)
    spread = jnp.mean(center * center, -1, keepdims=True)
    inverse = lax.rsqrt(spread + EPS)
    return (center * inverse, inverse)


def norm_back(grad_normed, normed, inverse):
    return inverse * (
        grad_normed
        - jnp.mean(grad_normed, -1, keepdims=True)
        - normed * jnp.mean(grad_normed * normed, -1, keepdims=True)
    )


def left_outer(left, right):
    return lax.dot_general(
        left, right, (((0,), (0,)), ((), ())), preferred_element_type=jnp.float32
    )


def right_outer(left, right):
    return lax.dot_general(
        left, right, (((1,), (1,)), ((), ())), preferred_element_type=jnp.float32
    )


def head_scores(query_part, key_part, query_ids, key_ids, factor):
    logits = (
        jnp.einsum("qhd,khd->hqk", query_part, key_part, preferred_element_type=jnp.float32)
        * factor
    )
    return jnp.where(key_ids[None, None, :] <= query_ids[None, :, None], logits, NEG)


def body(
    hidden_in,
    positions,
    languages,
    ln1_gain,
    ln1_bias,
    w_qkv,
    b_qkv,
    w_out,
    ln2_gain,
    ln2_bias,
    w_gate,
    w_up,
    w_down,
    cotangent,
):
    tokens = hidden_in[0].astype(jnp.float32)
    places = positions[0]
    shard_rows = tokens.shape[0]
    width = tokens.shape[1]
    seq_devices = lax.axis_size("seq")
    length = shard_rows * seq_devices
    position_here = lax.axis_index("seq")
    heads_count = width // HEAD_DIM
    group_heads = 4
    group_steps = heads_count // group_heads
    group_width = group_heads * HEAD_DIM
    factor = float(HEAD_DIM) ** (-0.5)
    language_ids = jnp.arange(LANGS, dtype=jnp.int32)
    marks_all = (languages[:, None] == language_ids[None, :]).astype(jnp.int32)
    language_totals = jnp.sum(marks_all, 0)
    own_language = lax.dynamic_slice_in_dim(languages, lax.axis_index("row"), 1, 0)
    own_marks = (own_language[0] == language_ids).astype(jnp.int32)
    own_count = jnp.sum(own_marks * language_totals)
    row_weight = jnp.float32(languages.shape[0] * length) / (
        LANGS * (own_count * length).astype(jnp.float32)
    )
    gain_one = ln1_gain.astype(jnp.float32)
    shift_one = ln1_bias.astype(jnp.float32)
    gain_two = ln2_gain.astype(jnp.float32)
    shift_two = ln2_bias.astype(jnp.float32)
    normed_one, inverse_one = standardize(tokens)
    first_in = (normed_one * gain_one + shift_one).astype(jnp.bfloat16)
    qkv_full, out_full, bias_full = (
        lax.all_gather(w_qkv, "seq", axis=1, tiled=True),
        lax.all_gather(w_out, "seq", axis=0, tiled=True),
        lax.all_gather(b_qkv, "seq", axis=0, tiled=True),
    )
    projected = jnp.dot(first_in, qkv_full, preferred_element_type=jnp.float32) + bias_full.astype(
        jnp.float32
    )
    head_shape = (shard_rows, heads_count, HEAD_DIM)
    queries = (
        rotate(projected[:, :width].reshape(head_shape), places, 1.0)
        .reshape(shard_rows, width)
        .astype(jnp.bfloat16)
    )
    keys_local = (
        rotate(projected[:, width : 2 * width].reshape(head_shape), places, 1.0)
        .reshape(shard_rows, width)
        .astype(jnp.bfloat16)
    )
    values_local = projected[:, 2 * width :].astype(jnp.bfloat16)
    keys_full, values_full = (
        lax.all_gather(keys_local, "seq", axis=0, tiled=True),
        lax.all_gather(values_local, "seq", axis=0, tiled=True),
    )
    query_ids = position_here * shard_rows + jnp.arange(shard_rows, dtype=jnp.int32)
    key_ids = jnp.arange(length, dtype=jnp.int32)

    def split_heads(matrix, column):
        return lax.dynamic_slice_in_dim(matrix, column, group_width, 1).reshape(
            matrix.shape[0], group_heads, HEAD_DIM
        )

    def attend_forward(number, carry):
        mixed_acc, stats = carry
        column = number * group_width
        logits = head_scores(
            split_heads(queries, column), split_heads(keys_full, column), query_ids, key_ids, factor
        )
        peak = jnp.max(logits, -1, keepdims=True)
        expo = jnp.exp(logits - peak)
        denom = jnp.sum(expo, -1, keepdims=True)
        probs = (expo / denom).astype(jnp.bfloat16)
        mixed_part = jnp.einsum(
            "hqk,khd->qhd",
            probs,
            split_heads(values_full, column),
            preferred_element_type=jnp.float32,
        )
        mixed_acc = lax.dynamic_update_slice_in_dim(
            mixed_acc, mixed_part.reshape(shard_rows, group_width), column, 1
        )
        stats = lax.dynamic_update_slice_in_dim(
            stats, (peak + jnp.log(denom))[..., 0], number * group_heads, 0
        )
        return (mixed_acc, stats)

    mixed_f, log_sums = lax.fori_loop(
        0,
        group_steps,
        attend_forward,
        (
            jnp.zeros((shard_rows, width), jnp.float32),
            jnp.zeros((heads_count, shard_rows), jnp.float32),
        ),
    )
    mixed = mixed_f.astype(jnp.bfloat16)
    middle = tokens + jnp.dot(mixed, out_full, preferred_element_type=jnp.float32)
    normed_two, inverse_two = standardize(middle)
    second_in = (normed_two * gain_two + shift_two).astype(jnp.bfloat16)
    second_full = lax.all_gather(second_in, "seq", axis=0, tiled=True)
    gate = jnp.dot(second_full, w_gate, preferred_element_type=jnp.float32)
    upward = jnp.dot(second_full, w_up, preferred_element_type=jnp.float32)
    sigmoid_gate = jax.nn.sigmoid(gate)
    activated = gate * sigmoid_gate
    hidden = (activated * upward).astype(jnp.bfloat16)
    feed_out = lax.psum_scatter(
        jnp.dot(hidden, w_down, preferred_element_type=jnp.float32).astype(jnp.bfloat16),
        "seq",
        scatter_dimension=0,
        tiled=True,
    ).astype(jnp.float32)
    output = (middle + feed_out).astype(jnp.bfloat16)[None]
    grad_top = cotangent[0].astype(jnp.float32) * row_weight
    grad_top_low = grad_top.astype(jnp.bfloat16)
    grad_top_full = lax.all_gather(grad_top_low, "seq", axis=0, tiled=True)
    grad_hidden = right_outer(grad_top_full, w_down)
    grad_w_down = left_outer(hidden, grad_top_full)
    slope = sigmoid_gate * (1.0 + gate * (1.0 - sigmoid_gate))
    grad_gate = (grad_hidden * upward * slope).astype(jnp.bfloat16)
    grad_upward = (grad_hidden * activated).astype(jnp.bfloat16)
    grad_w_gate = left_outer(second_full, grad_gate)
    grad_w_up = left_outer(second_full, grad_upward)
    grad_second = lax.psum_scatter(
        right_outer(grad_gate, w_gate) + right_outer(grad_upward, w_up),
        "seq",
        scatter_dimension=0,
        tiled=True,
    )
    grad_ln2_gain = jnp.sum(grad_second * normed_two, 0)
    grad_ln2_bias = jnp.sum(grad_second, 0)
    grad_middle = grad_top + norm_back(grad_second * gain_two, normed_two, inverse_two)
    grad_middle_low = grad_middle.astype(jnp.bfloat16)
    grad_w_out = left_outer(mixed, grad_middle_low)
    grad_mixed = right_outer(grad_middle_low, out_full).astype(jnp.bfloat16)

    def attend_back(number, carry):
        grad_query_acc, grad_key_acc, grad_value_acc = carry
        column = number * group_width
        query_part = split_heads(queries, column)
        key_part = split_heads(keys_full, column)
        grad_part = split_heads(grad_mixed, column)
        stats = lax.dynamic_slice_in_dim(log_sums, number * group_heads, group_heads, 0)
        logits = head_scores(query_part, key_part, query_ids, key_ids, factor)
        probs = jnp.exp(logits - stats[:, :, None])
        grad_probs = jnp.einsum(
            "qhd,khd->hqk",
            grad_part,
            split_heads(values_full, column),
            preferred_element_type=jnp.float32,
        )
        grad_values = jnp.einsum(
            "hqk,qhd->khd",
            probs.astype(jnp.bfloat16),
            grad_part,
            preferred_element_type=jnp.float32,
        )
        inner = jnp.sum(grad_probs * probs, -1, keepdims=True)
        grad_logits = (probs * (grad_probs - inner)).astype(jnp.bfloat16)
        grad_queries = (
            jnp.einsum("hqk,khd->qhd", grad_logits, key_part, preferred_element_type=jnp.float32)
            * factor
        )
        grad_keys = (
            jnp.einsum("hqk,qhd->khd", grad_logits, query_part, preferred_element_type=jnp.float32)
            * factor
        )
        key_sum, value_sum = (
            lax.psum_scatter(
                grad_keys.reshape(length, group_width), "seq", scatter_dimension=0, tiled=True
            ),
            lax.psum_scatter(
                grad_values.reshape(length, group_width), "seq", scatter_dimension=0, tiled=True
            ),
        )
        grad_query_acc = lax.dynamic_update_slice_in_dim(
            grad_query_acc, grad_queries.reshape(shard_rows, group_width), column, 1
        )
        grad_key_acc = lax.dynamic_update_slice_in_dim(grad_key_acc, key_sum, column, 1)
        grad_value_acc = lax.dynamic_update_slice_in_dim(grad_value_acc, value_sum, column, 1)
        return (grad_query_acc, grad_key_acc, grad_value_acc)

    empty = jnp.zeros((shard_rows, width), jnp.float32)
    grad_query_all, grad_key_all, grad_value_all = lax.fori_loop(
        0, group_steps, attend_back, (empty, empty, empty)
    )
    grad_query_turned = rotate(grad_query_all.reshape(head_shape), places, -1.0).reshape(
        shard_rows, width
    )
    grad_key_turned = rotate(grad_key_all.reshape(head_shape), places, -1.0).reshape(
        shard_rows, width
    )
    grad_projected = jnp.concatenate(
        [grad_query_turned, grad_key_turned, grad_value_all], 1
    ).astype(jnp.bfloat16)
    grad_w_qkv = left_outer(first_in, grad_projected)
    grad_b_qkv = jnp.sum(grad_projected.astype(jnp.float32), 0)
    grad_first = right_outer(grad_projected, qkv_full)
    grad_ln1_gain = jnp.sum(grad_first * normed_one, 0)
    grad_ln1_bias = jnp.sum(grad_first, 0)
    input_grad = (grad_middle + norm_back(grad_first * gain_one, normed_one, inverse_one)).astype(
        jnp.bfloat16
    )[None]
    seq_sums = (
        lax.psum_scatter(grad_ln1_gain, "seq", scatter_dimension=0, tiled=True),
        lax.psum_scatter(grad_ln1_bias, "seq", scatter_dimension=0, tiled=True),
        lax.psum_scatter(grad_w_qkv, "seq", scatter_dimension=1, tiled=True),
        lax.psum_scatter(grad_b_qkv, "seq", scatter_dimension=0, tiled=True),
        lax.psum_scatter(grad_w_out, "seq", scatter_dimension=0, tiled=True),
        lax.psum_scatter(grad_ln2_gain, "seq", scatter_dimension=0, tiled=True),
        lax.psum_scatter(grad_ln2_bias, "seq", scatter_dimension=0, tiled=True),
    )
    totals = lax.psum(
        (
            seq_sums[0],
            seq_sums[1],
            seq_sums[2],
            seq_sums[3],
            seq_sums[4],
            seq_sums[5],
            seq_sums[6],
            grad_w_gate,
            grad_w_up,
            grad_w_down,
        ),
        "row",
    )
    return (
        output,
        input_grad,
        totals[0],
        totals[1],
        totals[2],
        totals[3],
        totals[4],
        totals[5],
        totals[6],
        totals[7],
        totals[8],
        totals[9],
    )


def solution(mesh):
    placed = (
        P("row", "seq", None),
        P("row", "seq"),
        P(),
        P(),
        P(),
        P(None, "seq"),
        P("seq"),
        P("seq", None),
        P(),
        P(),
        P(None, "seq"),
        P(None, "seq"),
        P("seq", None),
        P("row", "seq", None),
    )
    return jax.shard_map(
        body,
        mesh=mesh,
        in_specs=placed,
        out_specs=(
            P("row", "seq", None),
            P("row", "seq", None),
            P("seq"),
            P("seq"),
            P(None, "seq"),
            P("seq"),
            P("seq", None),
            P("seq"),
            P("seq"),
            P(None, "seq"),
            P(None, "seq"),
            P("seq", None),
        ),
        check_vma=False,
    )
```

profile of v0, /device:TPU:0, one launch (start us, length us, event | category | flops | bytes accessed | tf_op | source)
XLA Modules:
  0.0 2399.7 jit_solution(3810746980370201801)
XLA Ops:
  24.4 207.9 %all-gather.8.cloned.1.call-done = bf16[2048,6144]{1,0:T(8,128)(2,1)} async-done(((bf16[2048,768]{1,0:T(8,128)(2,1)}), bf16[2048,6144]{1,0:T(8,128)(2,1)}) %all-gather.8.cloned.1.call-update) | async-done | bytes 25165840 | tf_op jit(solution)/shard_map/all_gather | solution.py:111
  263.6 26.6 %all-gather.10.cloned.1.call-done = bf16[1024,2048]{1,0:T(8,128)(2,1)} async-done(((bf16[128,2048]{1,0:T(8,128)(2,1)}), bf16[1024,2048]{1,0:T(8,128)(2,1)}) %all-gather.10.cloned.1.call-update) | async-done | bytes 4194320 | tf_op jit(solution)/shard_map/all_gather | solution.py:132
  296.5 42.4 %all-gather.12.cloned.1.call-done = bf16[1024,2048]{0,1:T(8,128)(2,1)} async-done(((bf16[128,2048]{0,1:T(8,128)(2,1)}), bf16[1024,2048]{0,1:T(8,128)(2,1)}) %all-gather.12.cloned.1.call-update) | async-done | bytes 4194320 | tf_op jit(solution)/shard_map/all_gather | solution.py:131
  339.0 39.6 %while.34 = (s32[]{:T(128)}, bf16[128,2048]{0,1:T(8,128)(2,1)}, f32[32,128]{1,0:T(8,128)S(1)}, bf16[1024,2048]{0,1:T(8,128)(2,1)}, bf16[128,2048]{0,1:T(8,128)(2...) while((s32[]{:T(128)}, bf16[128,2048]{0,1:T(8,128)(2,1)}, ...), condition=%wide.region_5.0_spmd.clone, body=%wide.region_2.5_spmd.clone.sunk | while | flops 140639872 | bytes 10372341 | solution.py:166
  378.6 42.1 %all-gather.14.cloned.1.call-done = bf16[2048,2048]{1,0:T(8,128)(2,1)} async-done(((bf16[256,2048]{1,0:T(8,128)(2,1)}), bf16[2048,2048]{1,0:T(8,128)(2,1)}) %all-gather.14.cloned.1.call-update) | async-done | bytes 8388624 | tf_op jit(solution)/shard_map/all_gather | solution.py:112
  431.9 41.3 %all-gather.16.cloned.1.call-done = bf16[1024,2048]{1,0:T(8,128)(2,1)} async-done(((bf16[128,2048]{1,0:T(8,128)(2,1)}), bf16[1024,2048]{1,0:T(8,128)(2,1)}) %all-gather.16.cloned.1.call-update) | async-done | bytes 4194320 | tf_op jit(solution)/shard_map/all_gather | solution.py:179
  486.0 35.0 %all-gather.18.cloned.1.call-done = bf16[1024,2048]{1,0:T(8,128)(2,1)} async-done(((bf16[128,2048]{1,0:T(8,128)(2,1)}), bf16[1024,2048]{1,0:T(8,128)(2,1)}) %all-gather.18.cloned.1.call-update) | async-done | bytes 4194320 | tf_op jit(solution)/shard_map/all_gather | solution.py:194
  545.9 81.8 %reduce-scatter.9.cloned.1.call-done = f32[128,2048]{1,0:T(8,128)} async-done(((f32[1024,2048]{1,0:T(8,128)}), f32[128,2048]{1,0:T(8,128)}) %reduce-scatter.9.cloned.1.call-update) | async-done | bytes 1048592 | tf_op jit(solution)/shard_map/reduce_scatter | solution.py:202
  629.3 49.6 %reduce-scatter.7.cloned.1.call-done = bf16[128,2048]{1,0:T(8,128)(2,1)} async-done(((bf16[1024,2048]{1,0:T(8,128)(2,1)}), bf16[128,2048]{1,0:T(8,128)(2,1)}) %reduce-scatter.7.cloned.1.call-update) | async-done | bytes 524304 | tf_op jit(solution)/shard_map/reduce_scatter | solution.py:185
  699.6 566.8 %while.35 = (s32[]{:T(128)}, f32[128,2048]{0,1:T(8,128)}, f32[128,2048]{0,1:T(8,128)}, bf16[128,2048]{0,1:T(8,128)(2,1)}, bf16[1024,2048]{0,1:T(8,128)(2,1)}, /*...) while((s32[]{:T(128)}, f32[128,2048]{0,1:T(8,128)}, ...), condition=%wide.region_18.0_spmd.clone, body=%wide.region_14.18_spmd.clone.sunk | while | flops 340688512 | bytes 36711860 | solution.py:262
  708.6 27.6 %reduce-scatter.15.cloned.1.call-done = f32[128,256]{0,1:T(8,128)} async-done(((f32[1024,256]{0,1:T(8,128)}), f32[128,256]{0,1:T(8,128)}) %reduce-scatter.15.cloned.1.call-update) | async-done | bytes 131088 | tf_op jit(solution)/shard_map/while/body/eval_jaxpr/reduce_scatter | solution.py:247
  737.8 31.3 %reduce-scatter.17.cloned.1.call-done = f32[128,256]{0,1:T(8,128)} async-done(((f32[1024,256]{0,1:T(8,128)}), f32[128,256]{0,1:T(8,128)}) %reduce-scatter.17.cloned.1.call-update) | async-done | bytes 131088 | tf_op jit(solution)/shard_map/while/body/eval_jaxpr/reduce_scatter | solution.py:250
  779.6 27.4 %reduce-scatter.15.cloned.1.call-done = f32[128,256]{0,1:T(8,128)} async-done(((f32[1024,256]{0,1:T(8,128)}), f32[128,256]{0,1:T(8,128)}) %reduce-scatter.15.cloned.1.call-update) | async-done | bytes 131088 | tf_op jit(solution)/shard_map/while/body/eval_jaxpr/reduce_scatter | solution.py:247
  808.6 31.3 %reduce-scatter.17.cloned.1.call-done = f32[128,256]{0,1:T(8,128)} async-done(((f32[1024,256]{0,1:T(8,128)}), f32[128,256]{0,1:T(8,128)}) %reduce-scatter.17.cloned.1.call-update) | async-done | bytes 131088 | tf_op jit(solution)/shard_map/while/body/eval_jaxpr/reduce_scatter | solution.py:250
  850.4 27.3 %reduce-scatter.15.cloned.1.call-done = f32[128,256]{0,1:T(8,128)} async-done(((f32[1024,256]{0,1:T(8,128)}), f32[128,256]{0,1:T(8,128)}) %reduce-scatter.15.cloned.1.call-update) | async-done | bytes 131088 | tf_op jit(solution)/shard_map/while/body/eval_jaxpr/reduce_scatter | solution.py:247
  879.3 31.4 %reduce-scatter.17.cloned.1.call-done = f32[128,256]{0,1:T(8,128)} async-done(((f32[1024,256]{0,1:T(8,128)}), f32[128,256]{0,1:T(8,128)}) %reduce-scatter.17.cloned.1.call-update) | async-done | bytes 131088 | tf_op jit(solution)/shard_map/while/body/eval_jaxpr/reduce_scatter | solution.py:250
  921.2 27.3 %reduce-scatter.15.cloned.1.call-done = f32[128,256]{0,1:T(8,128)} async-done(((f32[1024,256]{0,1:T(8,128)}), f32[128,256]{0,1:T(8,128)}) %reduce-scatter.15.cloned.1.call-update) | async-done | bytes 131088 | tf_op jit(solution)/shard_map/while/body/eval_jaxpr/reduce_scatter | solution.py:247
  950.1 31.4 %reduce-scatter.17.cloned.1.call-done = f32[128,256]{0,1:T(8,128)} async-done(((f32[1024,256]{0,1:T(8,128)}), f32[128,256]{0,1:T(8,128)}) %reduce-scatter.17.cloned.1.call-update) | async-done | bytes 131088 | tf_op jit(solution)/shard_map/while/body/eval_jaxpr/reduce_scatter | solution.py:250
  992.0 27.3 %reduce-scatter.15.cloned.1.call-done = f32[128,256]{0,1:T(8,128)} async-done(((f32[1024,256]{0,1:T(8,128)}), f32[128,256]{0,1:T(8,128)}) %reduce-scatter.15.cloned.1.call-update) | async-done | bytes 131088 | tf_op jit(solution)/shard_map/while/body/eval_jaxpr/reduce_scatter | solution.py:247
  1020.8 31.4 %reduce-scatter.17.cloned.1.call-done = f32[128,256]{0,1:T(8,128)} async-done(((f32[1024,256]{0,1:T(8,128)}), f32[128,256]{0,1:T(8,128)}) %reduce-scatter.17.cloned.1.call-update) | async-done | bytes 131088 | tf_op jit(solution)/shard_map/while/body/eval_jaxpr/reduce_scatter | solution.py:250
  1062.7 27.4 %reduce-scatter.15.cloned.1.call-done = f32[128,256]{0,1:T(8,128)} async-done(((f32[1024,256]{0,1:T(8,128)}), f32[128,256]{0,1:T(8,128)}) %reduce-scatter.15.cloned.1.call-update) | async-done | bytes 131088 | tf_op jit(solution)/shard_map/while/body/eval_jaxpr/reduce_scatter | solution.py:247
  1091.7 31.3 %reduce-scatter.17.cloned.1.call-done = f32[128,256]{0,1:T(8,128)} async-done(((f32[1024,256]{0,1:T(8,128)}), f32[128,256]{0,1:T(8,128)}) %reduce-scatter.17.cloned.1.call-update) | async-done | bytes 131088 | tf_op jit(solution)/shard_map/while/body/eval_jaxpr/reduce_scatter | solution.py:250
  1133.5 27.4 %reduce-scatter.15.cloned.1.call-done = f32[128,256]{0,1:T(8,128)} async-done(((f32[1024,256]{0,1:T(8,128)}), f32[128,256]{0,1:T(8,128)}) %reduce-scatter.15.cloned.1.call-update) | async-done | bytes 131088 | tf_op jit(solution)/shard_map/while/body/eval_jaxpr/reduce_scatter | solution.py:247
  1162.5 31.5 %reduce-scatter.17.cloned.1.call-done = f32[128,256]{0,1:T(8,128)} async-done(((f32[1024,256]{0,1:T(8,128)}), f32[128,256]{0,1:T(8,128)}) %reduce-scatter.17.cloned.1.call-update) | async-done | bytes 131088 | tf_op jit(solution)/shard_map/while/body/eval_jaxpr/reduce_scatter | solution.py:250
  1204.6 27.3 %reduce-scatter.15.cloned.1.call-done = f32[128,256]{0,1:T(8,128)} async-done(((f32[1024,256]{0,1:T(8,128)}), f32[128,256]{0,1:T(8,128)}) %reduce-scatter.15.cloned.1.call-update) | async-done | bytes 131088 | tf_op jit(solution)/shard_map/while/body/eval_jaxpr/reduce_scatter | solution.py:247
  1233.4 31.4 %reduce-scatter.17.cloned.1.call-done = f32[128,256]{0,1:T(8,128)} async-done(((f32[1024,256]{0,1:T(8,128)}), f32[128,256]{0,1:T(8,128)}) %reduce-scatter.17.cloned.1.call-update) | async-done | bytes 131088 | tf_op jit(solution)/shard_map/while/body/eval_jaxpr/reduce_scatter | solution.py:250
  1268.5 21.6 fusion.40
  1309.0 127.0 %reduce-scatter.13.cloned.1.call-done = f32[256,2048]{1,0:T(8,128)} async-done(((f32[2048,2048]{1,0:T(8,128)}), f32[256,2048]{1,0:T(8,128)}) %reduce-scatter.13.cloned.1.call-update) | async-done | bytes 2097168 | tf_op jit(solution)/shard_map/reduce_scatter | solution.py:287
  1436.0 483.8 %reduce-scatter.11.cloned.1.call-done = f32[2048,768]{1,0:T(8,128)} async-done(((f32[2048,6144]{1,0:T(8,128)}), f32[2048,768]{1,0:T(8,128)}) %reduce-scatter.11.cloned.1.call-update) | async-done | bytes 6291472 | tf_op jit(solution)/shard_map/reduce_scatter | solution.py:285
  1922.8 20.7 fusion.30
  1943.5 26.4 %all-reduce.5 = (f32[2048]{0:T(1024)S(1)}, f32[2048]{0:T(1024)S(1)}, f32[6144]{0:T(1024)S(1)}, f32[2048]{0:T(1024)S(1)}, f32[2048]{0:T(1024)S(1)}) all-reduce(f32[2048]{0:T(1024)S(1)} %get-tuple-element.455, f32[2048]{0:T(1024)S(1)} %get-tuple-element.460, ...), channel_id=6, replica_groups=mesh['row'=4,'seq'=8] {'seq'}, use_global_device_ids=true, to_apply=%region_22.23.clone | all-reduce | flops 14336 | bytes 114688
  1984.4 389.3 %all-reduce.10.cloned.1.call-done = (f32[2048,768]{1,0:T(8,128)}, f32[256,2048]{1,0:T(8,128)}, f32[2048,704]{0,1:T(8,128)}, f32[2048,704]{0,1:T(8,128)}, f32[704,2048]{1,0:T(8,128)}) async-done(((f32[2048,768]{1,0:T(8,128)}, f32[256,2048]{1,0:T(8,128)}, f32[2048,704]{0,1:T(8,128)}, f32[2048,704]{0,1:T(8,128)}, f32[704,2048]{1,0:T(8,128)}), (f32[2048,768]{1,0:T(8,128)}, f32[256,2048]{1,0:T(8,128)}, ...) | async-done | bytes 25690128 | tf_op jit(solution)/shard_map/psum | solution.py:291
  (452 shorter events, 316.4 us)
Async XLA Ops:
  7.2 513.8 %copy-start = (bf16[704,2048]{1,0:T(8,128)(2,1)S(1)}, bf16[704,2048]{1,0:T(8,128)(2,1)}, u32[]{:S(2)}) copy-start(bf16[704,2048]{1,0:T(8,128)(2,1)} %param.30) | copy-start | bytes 8650756
  7.2 225.0 %all-gather.8.cloned.1.call-start = ((), (), s32[]{:S(2)}) async-start(), calls=%async_computation.6 | async-start | bytes 28311552 | tf_op jit(solution)/shard_map/all_gather | solution.py:111
  8.0 282.2 %all-gather.10.cloned.1.call-start = ((), (), s32[]{:S(2)}) async-start(), calls=%async_computation.7 | async-start | bytes 4718592 | tf_op jit(solution)/shard_map/all_gather | solution.py:132
  244.9 94.0 %all-gather.12.cloned.1.call-start = ((), (), s32[]{:S(2)}) async-start(), calls=%async_computation.8 | async-start | bytes 4718592 | tf_op jit(solution)/shard_map/all_gather | solution.py:131
  257.2 163.4 %all-gather.14.cloned.1.call-start = ((), (), s32[]{:S(2)}) async-start(), calls=%async_computation.9 | async-start | bytes 9437184 | tf_op jit(solution)/shard_map/all_gather | solution.py:112
  257.8 215.4 %all-gather.16.cloned.1.call-start = ((), (), s32[]{:S(2)}) async-start(), calls=%async_computation.10 | async-start | bytes 4718592 | tf_op jit(solution)/shard_map/all_gather | solution.py:179
  427.7 93.3 %all-gather.18.cloned.1.call-start = ((), (), s32[]{:S(2)}) async-start(), calls=%async_computation.12 | async-start | bytes 4718592 | tf_op jit(solution)/shard_map/all_gather | solution.py:194
  431.4 196.3 %reduce-scatter.9.cloned.1.call-start = ((), (), s32[]{:S(2)}) async-start(), calls=%async_computation.13 | async-start | bytes 9437184 | tf_op jit(solution)/shard_map/reduce_scatter | solution.py:202
  539.2 139.8 %reduce-scatter.7.cloned.1.call-start = ((), (), s32[]{:S(2)}) async-start(), calls=%async_computation.11 | async-start | bytes 4718592 | tf_op jit(solution)/shard_map/reduce_scatter | solution.py:185
  545.8 81.8 %copy-start.4 = (f32[128,2048]{1,0:T(8,128)S(1)}, f32[128,2048]{1,0:T(8,128)}, u32[]{:S(2)}) copy-start(f32[128,2048]{1,0:T(8,128)} %copy-done.3) | copy-start | bytes 3145732
  699.6 36.6 %reduce-scatter.15.cloned.1.call-start = ((), (), s32[]{:S(2)}) async-start(), calls=%async_computation.17 | async-start | bytes 1179648 | tf_op jit(solution)/shard_map/while/body/eval_jaxpr/reduce_scatter | solution.py:247
  705.0 64.1 %reduce-scatter.17.cloned.1.call-start = ((), (), s32[]{:S(2)}) async-start(), calls=%async_computation.18 | async-start | bytes 1179648 | tf_op jit(solution)/shard_map/while/body/eval_jaxpr/reduce_scatter | solution.py:250
  706.3 64.4 %copy-start.17 = (bf16[128,2048]{1,0:T(8,128)(2,1)S(1)}, bf16[128,2048]{1,0:T(8,128)(2,1)}, u32[]{:S(2)}) copy-start(bf16[128,2048]{1,0:T(8,128)(2,1)} %copy-done.16) | copy-start | bytes 1572868 | tf_op jit(solution)/shard_map/while
  770.6 36.4 %reduce-scatter.15.cloned.1.call-start = ((), (), s32[]{:S(2)}) async-start(), calls=%async_computation.17 | async-start | bytes 1179648 | tf_op jit(solution)/shard_map/while/body/eval_jaxpr/reduce_scatter | solution.py:247
  776.0 63.8 %reduce-scatter.17.cloned.1.call-start = ((), (), s32[]{:S(2)}) async-start(), calls=%async_computation.18 | async-start | bytes 1179648 | tf_op jit(solution)/shard_map/while/body/eval_jaxpr/reduce_scatter | solution.py:250
  841.4 36.3 %reduce-scatter.15.cloned.1.call-start = ((), (), s32[]{:S(2)}) async-start(), calls=%async_computation.17 | async-start | bytes 1179648 | tf_op jit(solution)/shard_map/while/body/eval_jaxpr/reduce_scatter | solution.py:247
  846.8 63.8 %reduce-scatter.17.cloned.1.call-start = ((), (), s32[]{:S(2)}) async-start(), calls=%async_computation.18 | async-start | bytes 1179648 | tf_op jit(solution)/shard_map/while/body/eval_jaxpr/reduce_scatter | solution.py:250
  912.2 36.3 %reduce-scatter.15.cloned.1.call-start = ((), (), s32[]{:S(2)}) async-start(), calls=%async_computation.17 | async-start | bytes 1179648 | tf_op jit(solution)/shard_map/while/body/eval_jaxpr/reduce_scatter | solution.py:247
  917.6 63.8 %reduce-scatter.17.cloned.1.call-start = ((), (), s32[]{:S(2)}) async-start(), calls=%async_computation.18 | async-start | bytes 1179648 | tf_op jit(solution)/shard_map/while/body/eval_jaxpr/reduce_scatter | solution.py:250
  983.0 36.3 %reduce-scatter.15.cloned.1.call-start = ((), (), s32[]{:S(2)}) async-start(), calls=%async_computation.17 | async-start | bytes 1179648 | tf_op jit(solution)/shard_map/while/body/eval_jaxpr/reduce_scatter | solution.py:247
  988.4 63.8 %reduce-scatter.17.cloned.1.call-start = ((), (), s32[]{:S(2)}) async-start(), calls=%async_computation.18 | async-start | bytes 1179648 | tf_op jit(solution)/shard_map/while/body/eval_jaxpr/reduce_scatter | solution.py:250
  1053.8 36.4 %reduce-scatter.15.cloned.1.call-start = ((), (), s32[]{:S(2)}) async-start(), calls=%async_computation.17 | async-start | bytes 1179648 | tf_op jit(solution)/shard_map/while/body/eval_jaxpr/reduce_scatter | solution.py:247
  1059.1 63.9 %reduce-scatter.17.cloned.1.call-start = ((), (), s32[]{:S(2)}) async-start(), calls=%async_computation.18 | async-start | bytes 1179648 | tf_op jit(solution)/shard_map/while/body/eval_jaxpr/reduce_scatter | solution.py:250
  1124.6 36.4 %reduce-scatter.15.cloned.1.call-start = ((), (), s32[]{:S(2)}) async-start(), calls=%async_computation.17 | async-start | bytes 1179648 | tf_op jit(solution)/shard_map/while/body/eval_jaxpr/reduce_scatter | solution.py:247
  1130.0 64.1 %reduce-scatter.17.cloned.1.call-start = ((), (), s32[]{:S(2)}) async-start(), calls=%async_computation.18 | async-start | bytes 1179648 | tf_op jit(solution)/shard_map/while/body/eval_jaxpr/reduce_scatter | solution.py:250
  1131.3 64.3 %copy-start.17 = (bf16[128,2048]{1,0:T(8,128)(2,1)S(1)}, bf16[128,2048]{1,0:T(8,128)(2,1)}, u32[]{:S(2)}) copy-start(bf16[128,2048]{1,0:T(8,128)(2,1)} %copy-done.16) | copy-start | bytes 1572868 | tf_op jit(solution)/shard_map/while
  1195.6 36.3 %reduce-scatter.15.cloned.1.call-start = ((), (), s32[]{:S(2)}) async-start(), calls=%async_computation.17 | async-start | bytes 1179648 | tf_op jit(solution)/shard_map/while/body/eval_jaxpr/reduce_scatter | solution.py:247
  1201.0 63.9 %reduce-scatter.17.cloned.1.call-start = ((), (), s32[]{:S(2)}) async-start(), calls=%async_computation.18 | async-start | bytes 1179648 | tf_op jit(solution)/shard_map/while/body/eval_jaxpr/reduce_scatter | solution.py:250
  1202.3 64.1 %copy-start.17 = (bf16[128,2048]{1,0:T(8,128)(2,1)S(1)}, bf16[128,2048]{1,0:T(8,128)(2,1)}, u32[]{:S(2)}) copy-start(bf16[128,2048]{1,0:T(8,128)(2,1)} %copy-done.16) | copy-start | bytes 1572868 | tf_op jit(solution)/shard_map/while
  1266.4 169.6 %reduce-scatter.13.cloned.1.call-start = ((), (), s32[]{:S(2)}) async-start(), calls=%async_computation.15 | async-start | bytes 18874368 | tf_op jit(solution)/shard_map/reduce_scatter | solution.py:287
  1267.2 652.6 %reduce-scatter.11.cloned.1.call-start = ((), (), s32[]{:S(2)}) async-start(), calls=%async_computation.14 | async-start | bytes 56623104 | tf_op jit(solution)/shard_map/reduce_scatter | solution.py:285
  1290.1 1083.6 %all-reduce.10.cloned.1.call-start = ((), (), s32[]{:S(2)}) async-start(), calls=%async_computation.16 | async-start | bytes 51380224 | tf_op jit(solution)/shard_map/psum | solution.py:291
  (56 other events, 620.5 us)
Sparse Core Ops, SparseCore 0:
  9.7 222.5 all-gather.7
  245.1 45.0 all-gather.9
  292.3 46.6 all-gather.11
  340.4 80.2 all-gather.13
  427.8 45.3 all-gather.15
  475.3 45.6 all-gather.17
  539.3 88.3 reduce-scatter.8
  630.5 48.4 reduce-scatter.6
  705.1 31.0 reduce-scatter.14
  738.3 30.7 reduce-scatter.16
  776.2 30.7 reduce-scatter.14
  809.1 30.7 reduce-scatter.16
  846.9 30.7 reduce-scatter.14
  879.9 30.7 reduce-scatter.16
  917.7 30.7 reduce-scatter.14
  950.6 30.7 reduce-scatter.16
  988.5 30.7 reduce-scatter.14
  1021.4 30.7 reduce-scatter.16
  1059.3 30.7 reduce-scatter.14
  1092.2 30.7 reduce-scatter.16
  1130.1 30.7 reduce-scatter.14
  1163.2 30.7 reduce-scatter.16
  1201.1 30.7 reduce-scatter.14
  1234.0 30.7 reduce-scatter.16
  1269.5 166.3 reduce-scatter.12
  1438.2 481.5 reduce-scatter.10
  1924.5 449.1 all-reduce.9
where the time goes:
time: 2410 us; the launch traced here: 2400 us
  waiting for transfers between devices  2000 us (83%)
  matrix products  184 us (8%)
  local copies, waits for them, and re-layouts  117 us (5%)
  blocking collectives  53.7 us (2%)
  other arithmetic  26.4 us (1%)
    reduce_scatter x1, waiting for transfers between devices, body(): lax.psum_scatter(grad_w_qkv, 'seq', scatter_dimension=1, tiled=True)  484 us
    psum x1, waiting for transfers between devices, body(): lax.psum((seq_sums[0], seq_sums[1], seq_sums[2], seq_sums[3], seq_sums[4]...  389 us
    reduce_scatter x8, waiting for transfers between devices, attend_back(): lax.psum_scatter(grad_values.reshape(length, group_width), 'seq', scatter...  251 us
    reduce_scatter x8, waiting for transfers between devices, attend_back(): lax.psum_scatter(grad_keys.reshape(length, group_width), 'seq', scatter_d...  219 us
    all_gather x1, waiting for transfers between devices, body(): lax.all_gather(w_qkv, 'seq', axis=1, tiled=True)  208 us
    reduce_scatter x1, waiting for transfers between devices, body(): lax.psum_scatter(grad_w_out, 'seq', scatter_dimension=0, tiled=True)  127 us
    reduce_scatter x1, waiting for transfers between devices, body(): lax.psum_scatter(right_outer(grad_gate, w_gate) + right_outer(grad_upward...  81.8 us
    dot_general x5, matrix products, left_outer(): lax.dot_general(left, right, (((0,), (0,)), ((), ())), preferred_element_...  49.9 us
  transfers between devices with their start and end apart: 27, of which 27 were waited for; matrix products, arithmetic and copies ran while one was open for 8% of the time, Pallas kernels for 0%

commit v1 on v0

--- a/solution.py
+++ b/solution.py
@@ -9,6 +9,23 @@
 EPS = 1e-05
 NEG = -1e30
 BASE = 10000.0
+
+
+def return_all_steps_all_on_mesh(z_in):
+    z_new, now, g_now = (lax.axis_size("seq"), lax.axis_index("seq"), z_in.shape[1])
+    buffers = tuple(((q, (q + 1) % z_new) for q in range(z_new)))
+    main = jnp.zeros((*z_in.shape[:1], z_new * g_now, *z_in.shape[2:]), z_in.dtype)
+    main = lax.dynamic_update_slice_in_dim(main, z_in, now * g_now, axis=1)
+    wide_out = x_next = z_in
+    local_part = z_new // 2
+    table = tuple(((q, (q - 1) % z_new) for q in range(z_new)))
+    for i in range(1, local_part + 1):
+        wide_out = lax.ppermute(wide_out, "seq", buffers)
+        main = lax.dynamic_update_slice_in_dim(main, wide_out, (now - i) % z_new * g_now, axis=1)
+        if i < z_new - local_part:
+            x_next = lax.ppermute(x_next, "seq", table)
+            main = lax.dynamic_update_slice_in_dim(main, x_next, (now + i) % z_new * g_now, axis=1)
+    return main
 
 
 def rotate(tensor, places, direction):
@@ -108,7 +125,7 @@
     normed_one, inverse_one = standardize(tokens)
     first_in = (normed_one * gain_one + shift_one).astype(jnp.bfloat16)
     qkv_full, out_full, bias_full = (
-        lax.all_gather(w_qkv, "seq", axis=1, tiled=True),
+        return_all_steps_all_on_mesh(w_qkv),
         lax.all_gather(w_out, "seq", axis=0, tiled=True),
         lax.all_gather(b_qkv, "seq", axis=0, tiled=True),
     )

time: 2410 us -> 2490 us (1.033)
  local copies, waits for them, and re-layouts: 117 us -> 154 us
  blocking collectives: 53.7 us -> 87.5 us
    all_gather x1 -> x0, waiting for transfers between devices: 208 us -> none  [body(): lax.all_gather(w_qkv, 'seq', axis=1, tiled=True)]
    ppermute x0 -> x7, waiting for transfers between devices: none -> 195 us  [the longest x4 194 us: return_all_steps_all_on_mesh(): wide_out = lax.ppermute(wide_out, 'seq', buffers)]
    all_gather x1, blocking collectives: 15.8 us -> 49.6 us  [body(): lax.all_gather(b_qkv, 'seq', axis=0, tiled=True)]
  transfers between devices with their start and end apart: 27 -> 33, of which waited for: 27 -> 30; matrix products, arithmetic and copies ran while one was open for 8% -> 9% of each run, Pallas kernels for 0% -> 0%
where the time goes in v1:
time: 2490 us; the launch traced here: 2480 us
  waiting for transfers between devices  1990 us (80%)
  matrix products  188 us (8%)
  local copies, waits for them, and re-layouts  154 us (6%)
  blocking collectives  87.5 us (4%)
  other arithmetic  29.1 us (1%)
    reduce_scatter x1, waiting for transfers between devices, body(): lax.psum_scatter(grad_w_qkv, 'seq', scatter_dimension=1, tiled=True)  484 us
    psum x1, waiting for transfers between devices, body(): lax.psum((seq_sums[0], seq_sums[1], seq_sums[2], seq_sums[3], seq_sums[4]...  389 us
    reduce_scatter x8, waiting for transfers between devices, attend_back(): lax.psum_scatter(grad_values.reshape(length, group_width), 'seq', scatter...  252 us
    reduce_scatter x8, waiting for transfers between devices, attend_back(): lax.psum_scatter(grad_keys.reshape(length, group_width), 'seq', scatter_d...  218 us
    ppermute x4, waiting for transfers between devices, return_all_steps_all_on_mesh(): wide_out = lax.ppermute(wide_out, 'seq', buffers)  194 us
    reduce_scatter x1, waiting for transfers between devices, body(): lax.psum_scatter(grad_w_out, 'seq', scatter_dimension=0, tiled=True)  127 us
    reduce_scatter x1, waiting for transfers between devices, body(): lax.psum_scatter(right_outer(grad_gate, w_gate) + right_outer(grad_upward...  81.8 us
  transfers between devices with their start and end apart: 33, of which 30 were waited for; matrix products, arithmetic and copies ran while one was open for 9% of the time, Pallas kernels for 0%

profile of v1, /device:TPU:0, one launch (start us, length us, event | category | flops | bytes accessed | tf_op | source)
XLA Modules:
  0.0 2476.8 jit_solution(18127959643612547090)
XLA Ops:
  11.9 66.2 %collective-permute-done = bf16[2048,768]{1,0:T(8,128)(2,1)S(1)} collective-permute-done((bf16[2048,768]{1,0:T(8,128)(2,1)}, bf16[2048,768]{1,0:T(8,128)(2,1)S(1)}, u32[]{:S(2)}, u32[]{:S(2)}) %collective-permute-start) | collective-permute-done | bytes 3145760 | tf_op jit(solution)/shard_map/ppermute | solution.py:23
  83.3 65.3 %collective-permute-done.2 = bf16[2048,768]{1,0:T(8,128)(2,1)S(1)} collective-permute-done((bf16[2048,768]{1,0:T(8,128)(2,1)S(1)}, bf16[2048,768]{1,0:T(8,128)(2,1)S(1)}, u32[]{:S(2)}, u32[]{:S(2)}) %collective-permute-start.2) | collective-permute-done | bytes 3145760 | tf_op jit(solution)/shard_map/ppermute | solution.py:23
  152.7 63.0 %collective-permute-done.4 = bf16[2048,768]{1,0:T(8,128)(2,1)} collective-permute-done((bf16[2048,768]{1,0:T(8,128)(2,1)S(1)}, bf16[2048,768]{1,0:T(8,128)(2,1)}, u32[]{:S(2)}, u32[]{:S(2)}) %collective-permute-start.4) | collective-permute-done | bytes 3145760 | tf_op jit(solution)/shard_map/ppermute | solution.py:23
  216.4 49.6 %all-gather = bf16[8,1,768]{2,1,0:T(2,128)(2,1)S(1)} all-gather(bf16[1,1,768]{2,1,0:T(2,128)(2,1)S(1)} %reshape.337), channel_id=1, replica_groups=mesh['row'=4,'seq'=8] {'seq'}, dimensions={0}, use_global_device_ids=true | all-gather | bytes 13824 | tf_op jit(solution)/shard_map/all_gather | solution.py:130
  338.8 29.4 %all-gather.7.cloned.1.call-done = bf16[1024,2048]{1,0:T(8,128)(2,1)} async-done(((bf16[128,2048]{1,0:T(8,128)(2,1)}), bf16[1024,2048]{1,0:T(8,128)(2,1)}) %all-gather.7.cloned.1.call-update) | async-done | bytes 4194320 | tf_op jit(solution)/shard_map/all_gather | solution.py:149
  374.6 42.4 %all-gather.9.cloned.1.call-done = bf16[1024,2048]{0,1:T(8,128)(2,1)} async-done(((bf16[128,2048]{0,1:T(8,128)(2,1)}), bf16[1024,2048]{0,1:T(8,128)(2,1)}) %all-gather.9.cloned.1.call-update) | async-done | bytes 4194320 | tf_op jit(solution)/shard_map/all_gather | solution.py:148
  417.0 39.6 %while.34 = (s32[]{:T(128)}, bf16[128,2048]{0,1:T(8,128)(2,1)}, f32[32,128]{1,0:T(8,128)S(1)}, bf16[1024,2048]{0,1:T(8,128)(2,1)}, bf16[128,2048]{0,1:T(8,128)(2...) while((s32[]{:T(128)}, bf16[128,2048]{0,1:T(8,128)(2,1)}, ...), condition=%wide.region_5.6_spmd.clone, body=%wide.region_2.5_spmd.clone.sunk | while | flops 140639872 | bytes 10372341 | solution.py:183
  456.7 42.2 %all-gather.11.cloned.1.call-done = bf16[2048,2048]{1,0:T(8,128)(2,1)} async-done(((bf16[256,2048]{1,0:T(8,128)(2,1)}), bf16[2048,2048]{1,0:T(8,128)(2,1)}) %all-gather.11.cloned.1.call-update) | async-done | bytes 8388624 | tf_op jit(solution)/shard_map/all_gather | solution.py:129
  509.6 41.8 %all-gather.13.cloned.1.call-done = bf16[1024,2048]{1,0:T(8,128)(2,1)} async-done(((bf16[128,2048]{1,0:T(8,128)(2,1)}), bf16[1024,2048]{1,0:T(8,128)(2,1)}) %all-gather.13.cloned.1.call-update) | async-done | bytes 4194320 | tf_op jit(solution)/shard_map/all_gather | solution.py:196
  564.2 35.0 %all-gather.15.cloned.1.call-done = bf16[1024,2048]{1,0:T(8,128)(2,1)} async-done(((bf16[128,2048]{1,0:T(8,128)(2,1)}), bf16[1024,2048]{1,0:T(8,128)(2,1)}) %all-gather.15.cloned.1.call-update) | async-done | bytes 4194320 | tf_op jit(solution)/shard_map/all_gather | solution.py:211
  624.2 81.8 %reduce-scatter.9.cloned.1.call-done = f32[128,2048]{1,0:T(8,128)} async-done(((f32[1024,2048]{1,0:T(8,128)}), f32[128,2048]{1,0:T(8,128)}) %reduce-scatter.9.cloned.1.call-update) | async-done | bytes 1048592 | tf_op jit(solution)/shard_map/reduce_scatter | solution.py:219
  707.6 49.6 %reduce-scatter.7.cloned.1.call-done = bf16[128,2048]{1,0:T(8,128)(2,1)} async-done(((bf16[1024,2048]{1,0:T(8,128)(2,1)}), bf16[128,2048]{1,0:T(8,128)(2,1)}) %reduce-scatter.7.cloned.1.call-update) | async-done | bytes 524304 | tf_op jit(solution)/shard_map/reduce_scatter | solution.py:202
  777.8 567.7 %while.35 = (s32[]{:T(128)}, f32[128,2048]{0,1:T(8,128)}, f32[128,2048]{0,1:T(8,128)}, bf16[128,2048]{0,1:T(8,128)(2,1)}, bf16[1024,2048]{0,1:T(8,128)(2,1)}, /*...) while((s32[]{:T(128)}, f32[128,2048]{0,1:T(8,128)}, ...), condition=%wide.region_18.19_spmd.clone, body=%wide.region_14.0_spmd.clone.sunk | while | flops 340688512 | bytes 36711860 | solution.py:279
  786.8 27.5 %reduce-scatter.15.cloned.1.call-done = f32[128,256]{0,1:T(8,128)} async-done(((f32[1024,256]{0,1:T(8,128)}), f32[128,256]{0,1:T(8,128)}) %reduce-scatter.15.cloned.1.call-update) | async-done | bytes 131088 | tf_op jit(solution)/shard_map/while/body/eval_jaxpr/reduce_scatter | solution.py:264
  815.9 31.5 %reduce-scatter.17.cloned.1.call-done = f32[128,256]{0,1:T(8,128)} async-done(((f32[1024,256]{0,1:T(8,128)}), f32[128,256]{0,1:T(8,128)}) %reduce-scatter.17.cloned.1.call-update) | async-done | bytes 131088 | tf_op jit(solution)/shard_map/while/body/eval_jaxpr/reduce_scatter | solution.py:267
  858.1 27.2 %reduce-scatter.15.cloned.1.call-done = f32[128,256]{0,1:T(8,128)} async-done(((f32[1024,256]{0,1:T(8,128)}), f32[128,256]{0,1:T(8,128)}) %reduce-scatter.15.cloned.1.call-update) | async-done | bytes 131088 | tf_op jit(solution)/shard_map/while/body/eval_jaxpr/reduce_scatter | solution.py:264
  886.8 31.5 %reduce-scatter.17.cloned.1.call-done = f32[128,256]{0,1:T(8,128)} async-done(((f32[1024,256]{0,1:T(8,128)}), f32[128,256]{0,1:T(8,128)}) %reduce-scatter.17.cloned.1.call-update) | async-done | bytes 131088 | tf_op jit(solution)/shard_map/while/body/eval_jaxpr/reduce_scatter | solution.py:267
  929.0 27.3 %reduce-scatter.15.cloned.1.call-done = f32[128,256]{0,1:T(8,128)} async-done(((f32[1024,256]{0,1:T(8,128)}), f32[128,256]{0,1:T(8,128)}) %reduce-scatter.15.cloned.1.call-update) | async-done | bytes 131088 | tf_op jit(solution)/shard_map/while/body/eval_jaxpr/reduce_scatter | solution.py:264
  957.8 31.6 %reduce-scatter.17.cloned.1.call-done = f32[128,256]{0,1:T(8,128)} async-done(((f32[1024,256]{0,1:T(8,128)}), f32[128,256]{0,1:T(8,128)}) %reduce-scatter.17.cloned.1.call-update) | async-done | bytes 131088 | tf_op jit(solution)/shard_map/while/body/eval_jaxpr/reduce_scatter | solution.py:267
  1000.0 27.3 %reduce-scatter.15.cloned.1.call-done = f32[128,256]{0,1:T(8,128)} async-done(((f32[1024,256]{0,1:T(8,128)}), f32[128,256]{0,1:T(8,128)}) %reduce-scatter.15.cloned.1.call-update) | async-done | bytes 131088 | tf_op jit(solution)/shard_map/while/body/eval_jaxpr/reduce_scatter | solution.py:264
  1028.8 31.3 %reduce-scatter.17.cloned.1.call-done = f32[128,256]{0,1:T(8,128)} async-done(((f32[1024,256]{0,1:T(8,128)}), f32[128,256]{0,1:T(8,128)}) %reduce-scatter.17.cloned.1.call-update) | async-done | bytes 131088 | tf_op jit(solution)/shard_map/while/body/eval_jaxpr/reduce_scatter | solution.py:267
  1070.7 27.3 %reduce-scatter.15.cloned.1.call-done = f32[128,256]{0,1:T(8,128)} async-done(((f32[1024,256]{0,1:T(8,128)}), f32[128,256]{0,1:T(8,128)}) %reduce-scatter.15.cloned.1.call-update) | async-done | bytes 131088 | tf_op jit(solution)/shard_map/while/body/eval_jaxpr/reduce_scatter | solution.py:264
  1099.5 31.4 %reduce-scatter.17.cloned.1.call-done = f32[128,256]{0,1:T(8,128)} async-done(((f32[1024,256]{0,1:T(8,128)}), f32[128,256]{0,1:T(8,128)}) %reduce-scatter.17.cloned.1.call-update) | async-done | bytes 131088 | tf_op jit(solution)/shard_map/while/body/eval_jaxpr/reduce_scatter | solution.py:267
  1141.6 27.2 %reduce-scatter.15.cloned.1.call-done = f32[128,256]{0,1:T(8,128)} async-done(((f32[1024,256]{0,1:T(8,128)}), f32[128,256]{0,1:T(8,128)}) %reduce-scatter.15.cloned.1.call-update) | async-done | bytes 131088 | tf_op jit(solution)/shard_map/while/body/eval_jaxpr/reduce_scatter | solution.py:264
  1170.3 31.5 %reduce-scatter.17.cloned.1.call-done = f32[128,256]{0,1:T(8,128)} async-done(((f32[1024,256]{0,1:T(8,128)}), f32[128,256]{0,1:T(8,128)}) %reduce-scatter.17.cloned.1.call-update) | async-done | bytes 131088 | tf_op jit(solution)/shard_map/while/body/eval_jaxpr/reduce_scatter | solution.py:267
  1212.5 27.3 %reduce-scatter.15.cloned.1.call-done = f32[128,256]{0,1:T(8,128)} async-done(((f32[1024,256]{0,1:T(8,128)}), f32[128,256]{0,1:T(8,128)}) %reduce-scatter.15.cloned.1.call-update) | async-done | bytes 131088 | tf_op jit(solution)/shard_map/while/body/eval_jaxpr/reduce_scatter | solution.py:264
  1241.3 31.6 %reduce-scatter.17.cloned.1.call-done = f32[128,256]{0,1:T(8,128)} async-done(((f32[1024,256]{0,1:T(8,128)}), f32[128,256]{0,1:T(8,128)}) %reduce-scatter.17.cloned.1.call-update) | async-done | bytes 131088 | tf_op jit(solution)/shard_map/while/body/eval_jaxpr/reduce_scatter | solution.py:267
  1283.4 27.4 %reduce-scatter.15.cloned.1.call-done = f32[128,256]{0,1:T(8,128)} async-done(((f32[1024,256]{0,1:T(8,128)}), f32[128,256]{0,1:T(8,128)}) %reduce-scatter.15.cloned.1.call-update) | async-done | bytes 131088 | tf_op jit(solution)/shard_map/while/body/eval_jaxpr/reduce_scatter | solution.py:264
  1312.4 31.5 %reduce-scatter.17.cloned.1.call-done = f32[128,256]{0,1:T(8,128)} async-done(((f32[1024,256]{0,1:T(8,128)}), f32[128,256]{0,1:T(8,128)}) %reduce-scatter.17.cloned.1.call-update) | async-done | bytes 131088 | tf_op jit(solution)/shard_map/while/body/eval_jaxpr/reduce_scatter | solution.py:267
  1387.8 126.9 %reduce-scatter.13.cloned.1.call-done = f32[256,2048]{1,0:T(8,128)} async-done(((f32[2048,2048]{1,0:T(8,128)}), f32[256,2048]{1,0:T(8,128)}) %reduce-scatter.13.cloned.1.call-update) | async-done | bytes 2097168 | tf_op jit(solution)/shard_map/reduce_scatter | solution.py:304
  1514.6 483.9 %reduce-scatter.11.cloned.1.call-done = f32[2048,768]{1,0:T(8,128)} async-done(((f32[2048,6144]{1,0:T(8,128)}), f32[2048,768]{1,0:T(8,128)}) %reduce-scatter.11.cloned.1.call-update) | async-done | bytes 6291472 | tf_op jit(solution)/shard_map/reduce_scatter | solution.py:302
  2063.2 389.3 %all-reduce.10.cloned.1.call-done = (f32[2048,768]{1,0:T(8,128)}, f32[256,2048]{1,0:T(8,128)}, f32[2048,704]{0,1:T(8,128)}, f32[2048,704]{0,1:T(8,128)}, f32[704,2048]{1,0:T(8,128)}) async-done(((f32[2048,768]{1,0:T(8,128)}, f32[256,2048]{1,0:T(8,128)}, f32[2048,704]{0,1:T(8,128)}, f32[2048,704]{0,1:T(8,128)}, f32[704,2048]{1,0:T(8,128)}), (f32[2048,768]{1,0:T(8,128)}, f32[256,2048]{1,0:T(8,128)}, ...) | async-done | bytes 25690128 | tf_op jit(solution)/shard_map/psum | solution.py:308
  (480 shorter events, 422.4 us)
Async XLA Ops:
  7.2 361.0 %all-gather.7.cloned.1.call-start = ((), (), s32[]{:S(2)}) async-start(), calls=%async_computation.6 | async-start | bytes 4718592 | tf_op jit(solution)/shard_map/all_gather | solution.py:149
  7.2 70.8 %collective-permute-start = (bf16[2048,768]{1,0:T(8,128)(2,1)}, bf16[2048,768]{1,0:T(8,128)(2,1)S(1)}, u32[]{:S(2)}, u32[]{:S(2)}) collective-permute-start(bf16[2048,768]{1,0:T(8,128)(2,1)} %param.23), channel_id=1, source_target_pairs={{0,1},{1,2},{2,3},{3,4},{4,5},{5,6},{6,7},{7,0},{8,9},{9,10},{10,1... | collective-permute-start | bytes 9437192 | tf_op jit(solution)/shard_map/ppermute | solution.py:23
  7.8 72.0 %collective-permute-start.1 = (bf16[2048,768]{1,0:T(8,128)(2,1)}, bf16[2048,768]{1,0:T(8,128)(2,1)S(1)}, u32[]{:S(2)}, u32[]{:S(2)}) collective-permute-start(bf16[2048,768]{1,0:T(8,128)(2,1)} %param.23), channel_id=1, source_target_pairs={{0,7},{1,0},{2,1},{3,2},{4,3},{5,4},{6,5},{7,6},{8,15},{9,8},{10,9... | collective-permute-start | bytes 9437192 | tf_op jit(solution)/shard_map/ppermute | solution.py:26
  79.8 68.8 %collective-permute-start.2 = (bf16[2048,768]{1,0:T(8,128)(2,1)S(1)}, bf16[2048,768]{1,0:T(8,128)(2,1)S(1)}, u32[]{:S(2)}, u32[]{:S(2)}) collective-permute-start(bf16[2048,768]{1,0:T(8,128)(2,1)S(1)} %collective-permute-done), channel_id=1, source_target_pairs={{0,1},{1,2},{2,3},{3,4},{4,5},{5,6},{6,7},{7,0},{8,9},{9,10},{10,1... | collective-permute-start | bytes 9437192 | tf_op jit(solution)/shard_map/ppermute | solution.py:23
  79.8 69.1 %collective-permute-start.3 = (bf16[2048,768]{1,0:T(8,128)(2,1)S(1)}, bf16[2048,768]{1,0:T(8,128)(2,1)}, u32[]{:S(2)}, u32[]{:S(2)}) collective-permute-start(bf16[2048,768]{1,0:T(8,128)(2,1)S(1)} %collective-permute-done.1), channel_id=1, source_target_pairs={{0,7},{1,0},{2,1},{3,2},{4,3},{5,4},{6,5},{7,6},{8,15},{9,8},{10,9... | collective-permute-start | bytes 9437192 | tf_op jit(solution)/shard_map/ppermute | solution.py:26
  148.6 67.1 %collective-permute-start.4 = (bf16[2048,768]{1,0:T(8,128)(2,1)S(1)}, bf16[2048,768]{1,0:T(8,128)(2,1)}, u32[]{:S(2)}, u32[]{:S(2)}) collective-permute-start(bf16[2048,768]{1,0:T(8,128)(2,1)S(1)} %collective-permute-done.2), channel_id=1, source_target_pairs={{0,1},{1,2},{2,3},{3,4},{4,5},{5,6},{6,7},{7,0},{8,9},{9,10},{10,1... | collective-permute-start | bytes 9437192 | tf_op jit(solution)/shard_map/ppermute | solution.py:23
  150.2 147.2 %collective-permute-start.5 = (bf16[2048,768]{1,0:T(8,128)(2,1)}, bf16[2048,768]{1,0:T(8,128)(2,1)}, u32[]{:S(2)}, u32[]{:S(2)}) collective-permute-start(bf16[2048,768]{1,0:T(8,128)(2,1)} %collective-permute-done.3), channel_id=1, source_target_pairs={{0,7},{1,0},{2,1},{3,2},{4,3},{5,4},{6,5},{7,6},{8,15},{9,8},{10,9... | collective-permute-start | bytes 9437192 | tf_op jit(solution)/shard_map/ppermute | solution.py:26
  215.7 85.7 %collective-permute-start.6 = (bf16[2048,768]{1,0:T(8,128)(2,1)}, bf16[2048,768]{1,0:T(8,128)(2,1)}, u32[]{:S(2)}, u32[]{:S(2)}) collective-permute-start(bf16[2048,768]{1,0:T(8,128)(2,1)} %collective-permute-done.4), channel_id=1, source_target_pairs={{0,1},{1,2},{2,3},{3,4},{4,5},{5,6},{6,7},{7,0},{8,9},{9,10},{10,1... | collective-permute-start | bytes 9437192 | tf_op jit(solution)/shard_map/ppermute | solution.py:23
  320.8 96.3 %all-gather.9.cloned.1.call-start = ((), (), s32[]{:S(2)}) async-start(), calls=%async_computation.7 | async-start | bytes 4718592 | tf_op jit(solution)/shard_map/all_gather | solution.py:148
  333.3 165.6 %all-gather.11.cloned.1.call-start = ((), (), s32[]{:S(2)}) async-start(), calls=%async_computation.8 | async-start | bytes 9437184 | tf_op jit(solution)/shard_map/all_gather | solution.py:129
  334.0 217.5 %all-gather.13.cloned.1.call-start = ((), (), s32[]{:S(2)}) async-start(), calls=%async_computation.9 | async-start | bytes 4718592 | tf_op jit(solution)/shard_map/all_gather | solution.py:196
  506.0 93.3 %all-gather.15.cloned.1.call-start = ((), (), s32[]{:S(2)}) async-start(), calls=%async_computation.11 | async-start | bytes 4718592 | tf_op jit(solution)/shard_map/all_gather | solution.py:211
  509.6 196.4 %reduce-scatter.9.cloned.1.call-start = ((), (), s32[]{:S(2)}) async-start(), calls=%async_computation.12 | async-start | bytes 9437184 | tf_op jit(solution)/shard_map/reduce_scatter | solution.py:219
  617.4 139.8 %reduce-scatter.7.cloned.1.call-start = ((), (), s32[]{:S(2)}) async-start(), calls=%async_computation.10 | async-start | bytes 4718592 | tf_op jit(solution)/shard_map/reduce_scatter | solution.py:202
  777.8 36.6 %reduce-scatter.15.cloned.1.call-start = ((), (), s32[]{:S(2)}) async-start(), calls=%async_computation.16 | async-start | bytes 1179648 | tf_op jit(solution)/shard_map/while/body/eval_jaxpr/reduce_scatter | solution.py:264
  783.2 64.3 %reduce-scatter.17.cloned.1.call-start = ((), (), s32[]{:S(2)}) async-start(), calls=%async_computation.17 | async-start | bytes 1179648 | tf_op jit(solution)/shard_map/while/body/eval_jaxpr/reduce_scatter | solution.py:267
  849.0 36.3 %reduce-scatter.15.cloned.1.call-start = ((), (), s32[]{:S(2)}) async-start(), calls=%async_computation.16 | async-start | bytes 1179648 | tf_op jit(solution)/shard_map/while/body/eval_jaxpr/reduce_scatter | solution.py:264
  854.4 64.0 %reduce-scatter.17.cloned.1.call-start = ((), (), s32[]{:S(2)}) async-start(), calls=%async_computation.17 | async-start | bytes 1179648 | tf_op jit(solution)/shard_map/while/body/eval_jaxpr/reduce_scatter | solution.py:267
  919.9 36.3 %reduce-scatter.15.cloned.1.call-start = ((), (), s32[]{:S(2)}) async-start(), calls=%async_computation.16 | async-start | bytes 1179648 | tf_op jit(solution)/shard_map/while/body/eval_jaxpr/reduce_scatter | solution.py:264
  925.3 64.1 %reduce-scatter.17.cloned.1.call-start = ((), (), s32[]{:S(2)}) async-start(), calls=%async_computation.17 | async-start | bytes 1179648 | tf_op jit(solution)/shard_map/while/body/eval_jaxpr/reduce_scatter | solution.py:267
  990.9 36.3 %reduce-scatter.15.cloned.1.call-start = ((), (), s32[]{:S(2)}) async-start(), calls=%async_computation.16 | async-start | bytes 1179648 | tf_op jit(solution)/shard_map/while/body/eval_jaxpr/reduce_scatter | solution.py:264
  996.3 63.8 %reduce-scatter.17.cloned.1.call-start = ((), (), s32[]{:S(2)}) async-start(), calls=%async_computation.17 | async-start | bytes 1179648 | tf_op jit(solution)/shard_map/while/body/eval_jaxpr/reduce_scatter | solution.py:267
  1061.6 36.3 %reduce-scatter.15.cloned.1.call-start = ((), (), s32[]{:S(2)}) async-start(), calls=%async_computation.16 | async-start | bytes 1179648 | tf_op jit(solution)/shard_map/while/body/eval_jaxpr/reduce_scatter | solution.py:264
  1067.0 63.9 %reduce-scatter.17.cloned.1.call-start = ((), (), s32[]{:S(2)}) async-start(), calls=%async_computation.17 | async-start | bytes 1179648 | tf_op jit(solution)/shard_map/while/body/eval_jaxpr/reduce_scatter | solution.py:267
  1137.9 64.0 %reduce-scatter.17.cloned.1.call-start = ((), (), s32[]{:S(2)}) async-start(), calls=%async_computation.17 | async-start | bytes 1179648 | tf_op jit(solution)/shard_map/while/body/eval_jaxpr/reduce_scatter | solution.py:267
  1203.4 36.3 %reduce-scatter.15.cloned.1.call-start = ((), (), s32[]{:S(2)}) async-start(), calls=%async_computation.16 | async-start | bytes 1179648 | tf_op jit(solution)/shard_map/while/body/eval_jaxpr/reduce_scatter | solution.py:264
  1208.8 64.1 %reduce-scatter.17.cloned.1.call-start = ((), (), s32[]{:S(2)}) async-start(), calls=%async_computation.17 | async-start | bytes 1179648 | tf_op jit(solution)/shard_map/while/body/eval_jaxpr/reduce_scatter | solution.py:267
  1274.4 36.4 %reduce-scatter.15.cloned.1.call-start = ((), (), s32[]{:S(2)}) async-start(), calls=%async_computation.16 | async-start | bytes 1179648 | tf_op jit(solution)/shard_map/while/body/eval_jaxpr/reduce_scatter | solution.py:264
  1279.8 64.2 %reduce-scatter.17.cloned.1.call-start = ((), (), s32[]{:S(2)}) async-start(), calls=%async_computation.17 | async-start | bytes 1179648 | tf_op jit(solution)/shard_map/while/body/eval_jaxpr/reduce_scatter | solution.py:267
  1345.5 169.1 %reduce-scatter.13.cloned.1.call-start = ((), (), s32[]{:S(2)}) async-start(), calls=%async_computation.14 | async-start | bytes 18874368 | tf_op jit(solution)/shard_map/reduce_scatter | solution.py:304
  1346.1 652.4 %reduce-scatter.11.cloned.1.call-start = ((), (), s32[]{:S(2)}) async-start(), calls=%async_computation.13 | async-start | bytes 56623104 | tf_op jit(solution)/shard_map/reduce_scatter | solution.py:302
  1369.1 1083.4 %all-reduce.10.cloned.1.call-start = ((), (), s32[]{:S(2)}) async-start(), calls=%async_computation.15 | async-start | bytes 51380224 | tf_op jit(solution)/shard_map/psum | solution.py:308
  (66 other events, 1569.5 us)
Sparse Core Ops, SparseCore 0:
  320.9 47.3 all-gather.6
  370.4 46.6 all-gather.8
  418.7 80.2 all-gather.10
  506.1 45.3 all-gather.12
  553.5 45.6 all-gather.14
  617.6 88.3 reduce-scatter.8
  708.8 48.3 reduce-scatter.6
  783.3 31.0 reduce-scatter.14
  816.7 30.7 reduce-scatter.16
  854.5 30.7 reduce-scatter.14
  887.6 30.7 reduce-scatter.16
  925.4 30.7 reduce-scatter.14
  958.5 30.8 reduce-scatter.16
  996.4 30.7 reduce-scatter.14
  1029.3 30.7 reduce-scatter.16
  1067.1 30.7 reduce-scatter.14
  1100.1 30.8 reduce-scatter.16
  1138.0 30.7 reduce-scatter.14
  1171.1 30.7 reduce-scatter.16
  1208.9 30.7 reduce-scatter.14
  1242.0 30.7 reduce-scatter.16
  1279.9 30.9 reduce-scatter.14
  1313.1 30.7 reduce-scatter.16
  1348.4 166.2 reduce-scatter.12
  1517.0 481.4 reduce-scatter.10
  2003.3 449.1 all-reduce.9
